TPU v7x, 32 devices: a whole 2x2x4 slice. The times are simulated.
32 devices in a mesh: kpt: 2 (over y), pert: 4 (over z), pw: 4 (over x, core).
Axes of the slice: x: 2, y: 2, z: 4, core: 2. Of those that a mesh axis runs over, the one named last changes fastest.
Arguments:
- occupied: bfloat16 [3072, 8192], P(('kpt', 'pert'), 'pw'), parts along dimension 0, may hold values from -0.0625 to 0.0625
- response: bfloat16 [8, 128, 8192], P(('kpt', 'pert'), None, 'pw'), parts along dimension 0, may hold values from -6 to 6
Outputs:
- correlation: float32 [8, 128, 1536], P(('kpt', 'pert')), parts along dimension 0
- projected: float32 [8, 128, 8192], P(('kpt', 'pert'), None, 'pw'), parts along dimension 0
There are 2 independent parts, one for each index of `kpt`. A program takes and returns all parts, laid end to end along the dimension named above; each array names one. Nothing has to cross between parts.
All inputs are finite; a program needn't handle non-finite values.
Results may differ from a plain program's by a relative error of at most 0.00096.
Values may be sent and summed in bfloat16 or wider, within the bound.
No kernel may reach another device: no remote copies, remote signals or barrier semaphores. Data moves between devices by JAX's collectives and lax.ppermute only.
A program may use at most 64 MiB of HBM per device.

v0:
```python
import jax
import jax.numpy as jnp
from jax import lax
from jax.sharding import PartitionSpec as P


def from_behind(block, axis, distance):
    devices = range(lax.axis_size(axis))
    route = [((i - distance) % len(devices), i) for i in devices]
    return lax.ppermute(block, axis, route)


def local(occupied, response):
    rows = response.reshape(-1, response.shape[-1])
    band_local = occupied.shape[0]
    cycle_size = lax.axis_size("pert")
    total_bands = band_local * cycle_size
    zero_index = jnp.zeros((), jnp.int32)
    empty_correlation = jnp.zeros((rows.shape[0], total_bands), jnp.float32)
    empty_correction = jnp.zeros(rows.shape, jnp.float32)
    position = lax.axis_index("pert")

    def visit(step, piece, correlation, correction):
        owner = (position - step) % cycle_size
        start = owner * band_local
        part = lax.dot_general(
            rows, piece, (((1,), (1,)), ((), ())), preferred_element_type=jnp.float32
        )
        summed = lax.psum(part, "pw")
        correlation = lax.dynamic_update_slice(correlation, summed, (zero_index, start))
        correction = correction + jnp.dot(
            summed.astype(jnp.bfloat16), piece, preferred_element_type=jnp.float32
        )
        return (correlation, correction)

    def turn(step, state):
        piece, correlation, correction = state
        correlation, correction = visit(step, piece, correlation, correction)
        piece = from_behind(piece, "pert", 1)
        return (piece, correlation, correction)

    piece, correlation, correction = lax.fori_loop(
        0, cycle_size - 1, turn, (occupied, empty_correlation, empty_correction)
    )
    correlation, correction = visit(cycle_size - 1, piece, correlation, correction)
    projected = rows.astype(jnp.float32) - correction
    correlation_out = correlation.reshape(response.shape[0], response.shape[1], total_bands)
    return (correlation_out, projected.reshape(response.shape))


def solution(mesh):
    in_specs = (P(("kpt", "pert"), "pw"), P(("kpt", "pert"), None, "pw"))
    out_specs = (P(("kpt", "pert"), None, None), P(("kpt", "pert"), None, "pw"))
    return jax.shard_map(local, mesh=mesh, in_specs=in_specs, out_specs=out_specs, check_vma=False)
```

profile of v0, /device:TPU:0, one launch (start us, length us, event | category | flops | bytes accessed | tf_op | source)
XLA Modules:
  0.0 176.5 jit_solution(3041188094833959325)
XLA Ops:
  8.0 1.0 broadcast_in_dim.6
  9.0 0.7 copy-done
  9.7 120.9 %while.20 = (s32[]{:T(128)}, bf16[384,2048]{1,0:T(8,128)(2,1)S(1)}, f32[128,1536]{1,0:T(8,128)}, f32[128,2048]{1,0:T(8,128)}, bf16[128,2048]{1,0:T(8,128)(2,1)},...) while((s32[]{:T(128)}, bf16[384,2048]{1,0:T(8,128)(2,1)S(1)}, ...), condition=%wide.region_2.3_spmd.clone, body=%wide.region_0.2_spmd.clone.sunk | while | flops 403275776 | bytes 19267988 | solution.py:42
  9.9 3.1 %collective-permute-start = (bf16[384,2048]{1,0:T(8,128)(2,1)S(1)}, bf16[384,2048]{1,0:T(8,128)(2,1)S(1)}, u32[]{:S(2)}, u32[]{:S(2)}) collective-permute-start(bf16[384,2048]{1,0:T(8,128)(2,1)S(1)} %copy.12), channel_id=1, source_target_pairs={{12,0},{0,4},{4,8},{8,12},{13,1},{1,5},{5,9},{9,13},{14,2},{2,6},{... | collective-permute-start | bytes 4718600 | tf_op jit(solution)/shard_map/while/body/eval_jaxpr/ppermute | solution.py:10
  13.0 1.3 fusion.20
  14.3 33.2 %all-reduce.5.cloned.1.call-done = f32[128,384]{1,0:T(8,128)} async-done(((f32[128,384]{1,0:T(8,128)}), f32[128,384]{1,0:T(8,128)}) %all-reduce.5.cloned.1.call-update) | async-done | bytes 196624 | tf_op jit(solution)/shard_map/while/body/eval_jaxpr/psum | solution.py:29
  47.6 1.6 constant_dynamic-update-slice_fusion.3
  49.2 2.3 %convolution_add_fusion.3 = f32[128,2048]{1,0:T(8,128)} fusion(bf16[384,2048]{1,0:T(8,128)(2,1)S(1)} %copy.12, f32[128,2048]{1,0:T(8,128)} %get-tuple-element.247, pred[]{:T(512)S(6)} %compare.5, f32[128,384]{1,0:T(8,128)} %all-reduce.5.cloned.1.call-done), kind=kOutput, calls=%fused_computation.clone.1 | convolution fusion | flops 201900032 | bytes 3866625 | tf_op jit(solution)/shard_map/while/body/eval_jaxpr/dot_general | solution.py:31
  51.5 0.2 copy.12
  51.7 1.5 collective-permute-start
  53.2 1.3 fusion.20
  54.6 32.1 %all-reduce.5.cloned.1.call-done = f32[128,384]{1,0:T(8,128)} async-done(((f32[128,384]{1,0:T(8,128)}), f32[128,384]{1,0:T(8,128)}) %all-reduce.5.cloned.1.call-update) | async-done | bytes 196624 | tf_op jit(solution)/shard_map/while/body/eval_jaxpr/psum | solution.py:29
  86.7 1.6 constant_dynamic-update-slice_fusion.3
  88.3 2.8 %convolution_add_fusion.3 = f32[128,2048]{1,0:T(8,128)} fusion(bf16[384,2048]{1,0:T(8,128)(2,1)S(1)} %copy.12, f32[128,2048]{1,0:T(8,128)} %get-tuple-element.247, pred[]{:T(512)S(6)} %compare.5, f32[128,384]{1,0:T(8,128)} %all-reduce.5.cloned.1.call-done), kind=kOutput, calls=%fused_computation.clone.1 | convolution fusion | flops 201900032 | bytes 3866625 | tf_op jit(solution)/shard_map/while/body/eval_jaxpr/dot_general | solution.py:31
  91.3 1.5 collective-permute-start
  92.8 1.3 fusion.20
  94.2 32.1 %all-reduce.5.cloned.1.call-done = f32[128,384]{1,0:T(8,128)} async-done(((f32[128,384]{1,0:T(8,128)}), f32[128,384]{1,0:T(8,128)}) %all-reduce.5.cloned.1.call-update) | async-done | bytes 196624 | tf_op jit(solution)/shard_map/while/body/eval_jaxpr/psum | solution.py:29
  126.3 1.6 constant_dynamic-update-slice_fusion.3
  127.9 2.8 %convolution_add_fusion.3 = f32[128,2048]{1,0:T(8,128)} fusion(bf16[384,2048]{1,0:T(8,128)(2,1)S(1)} %copy.12, f32[128,2048]{1,0:T(8,128)} %get-tuple-element.247, pred[]{:T(512)S(6)} %compare.5, f32[128,384]{1,0:T(8,128)} %all-reduce.5.cloned.1.call-done), kind=kOutput, calls=%fused_computation.clone.1 | convolution fusion | flops 201900032 | bytes 3866625 | tf_op jit(solution)/shard_map/while/body/eval_jaxpr/dot_general | solution.py:31
  130.7 2.4 %convolution_bitcast_fusion = f32[128,384]{0,1:T(8,128)} fusion(bf16[384,2048]{1,0:T(8,128)(2,1)S(1)} %get-tuple-element.160, bf16[1,128,2048]{2,1,0:T(8,128)(2,1)} %bitcast.22), kind=kOutput, calls=%fused_computation.6 | convolution fusion | flops 201326592 | bytes 2293760 | tf_op jit(solution)/shard_map/dot_general | solution.py:26
  133.1 32.1 %all-reduce.3.cloned.1.call-done = f32[128,384]{0,1:T(8,128)} async-done(((f32[128,384]{0,1:T(8,128)}), f32[128,384]{0,1:T(8,128)}) %all-reduce.3.cloned.1.call-update) | async-done | bytes 196624 | tf_op jit(solution)/shard_map/psum | solution.py:29
  165.3 1.1 copy.4
  166.3 0.7 constant_dynamic-update-slice_fusion.1
  167.0 2.4 %fusion.2 = f32[1,128,2048]{2,1,0:T(8,128)} fusion(f32[128,2048]{1,0:T(8,128)S(1)} %copy-done.1, bf16[384,2048]{1,0:T(8,128)(2,1)S(1)} %get-tuple-element.160, f32[128,384]{0,1:T(8,128)} %all-reduce.3.cloned.1.call-done, bf16[1,128,2048]{2,1,0:T(8,128)(2,1)S(1)} %bitcast.23), kind=kOutput, calls=%fused_computation.5 | convolution fusion | flops 202162176 | bytes 4390912 | tf_op jit(solution)/shard_map/dot_general | solution.py:31
  (25 shorter events, 0.4 us)
Async XLA Ops:
  8.0 1.7 copy-start
  9.7 37.9 %all-reduce.5.cloned.1.call-start = ((), (), s32[]{:S(2)}) async-start(), calls=%async_computation.1 | async-start | bytes 393216 | tf_op jit(solution)/shard_map/while/body/eval_jaxpr/psum | solution.py:29
  9.7 3.3 %copy-start.2 = (bf16[128,2048]{1,0:T(8,128)(2,1)S(1)}, bf16[128,2048]{1,0:T(8,128)(2,1)}, u32[]{:S(2)}) copy-start(bf16[128,2048]{1,0:T(8,128)(2,1)} %get-tuple-element.260) | copy-start | bytes 1572868 | tf_op jit(solution)/shard_map/while
  9.9 41.7 %collective-permute-start = (bf16[384,2048]{1,0:T(8,128)(2,1)S(1)}, bf16[384,2048]{1,0:T(8,128)(2,1)S(1)}, u32[]{:S(2)}, u32[]{:S(2)}) collective-permute-start(bf16[384,2048]{1,0:T(8,128)(2,1)S(1)} %copy.12), channel_id=1, source_target_pairs={{12,0},{0,4},{4,8},{8,12},{13,1},{1,5},{5,9},{9,13},{14,2},{2,6},{... | collective-permute-start | bytes 4718600 | tf_op jit(solution)/shard_map/while/body/eval_jaxpr/ppermute | solution.py:10
  51.5 35.2 %all-reduce.5.cloned.1.call-start = ((), (), s32[]{:S(2)}) async-start(), calls=%async_computation.1 | async-start | bytes 393216 | tf_op jit(solution)/shard_map/while/body/eval_jaxpr/psum | solution.py:29
  51.5 1.7 copy-start.2
  51.7 39.4 %collective-permute-start = (bf16[384,2048]{1,0:T(8,128)(2,1)S(1)}, bf16[384,2048]{1,0:T(8,128)(2,1)S(1)}, u32[]{:S(2)}, u32[]{:S(2)}) collective-permute-start(bf16[384,2048]{1,0:T(8,128)(2,1)S(1)} %copy.12), channel_id=1, source_target_pairs={{12,0},{0,4},{4,8},{8,12},{13,1},{1,5},{5,9},{9,13},{14,2},{2,6},{... | collective-permute-start | bytes 4718600 | tf_op jit(solution)/shard_map/while/body/eval_jaxpr/ppermute | solution.py:10
  91.1 35.2 %all-reduce.5.cloned.1.call-start = ((), (), s32[]{:S(2)}) async-start(), calls=%async_computation.1 | async-start | bytes 393216 | tf_op jit(solution)/shard_map/while/body/eval_jaxpr/psum | solution.py:29
  91.1 1.7 copy-start.2
  91.3 39.4 %collective-permute-start = (bf16[384,2048]{1,0:T(8,128)(2,1)S(1)}, bf16[384,2048]{1,0:T(8,128)(2,1)S(1)}, u32[]{:S(2)}, u32[]{:S(2)}) collective-permute-start(bf16[384,2048]{1,0:T(8,128)(2,1)S(1)} %copy.12), channel_id=1, source_target_pairs={{12,0},{0,4},{4,8},{8,12},{13,1},{1,5},{5,9},{9,13},{14,2},{2,6},{... | collective-permute-start | bytes 4718600 | tf_op jit(solution)/shard_map/while/body/eval_jaxpr/ppermute | solution.py:10
  130.6 34.6 %all-reduce.3.cloned.1.call-start = ((), (), s32[]{:S(2)}) async-start(), calls=%async_computation | async-start | bytes 393216 | tf_op jit(solution)/shard_map/psum | solution.py:29
  130.6 36.4 %copy-start.1 = (f32[128,2048]{1,0:T(8,128)S(1)}, f32[128,2048]{1,0:T(8,128)}, u32[]{:S(2)}) copy-start(f32[128,2048]{1,0:T(8,128)} %get-tuple-element.161) | copy-start | bytes 3145732
  130.6 36.4 %copy-start.3 = (bf16[128,2048]{1,0:T(8,128)(2,1)S(1)}, bf16[128,2048]{1,0:T(8,128)(2,1)}, u32[]{:S(2)}) copy-start(bf16[128,2048]{1,0:T(8,128)(2,1)} %get-tuple-element.272) | copy-start | bytes 1572868
Sparse Core Ops, SparseCore 0:
  14.4 33.0 all-reduce.4
  54.7 31.9 all-reduce.4
  94.2 31.9 all-reduce.4
Sparse Core Ops, SparseCore 1:
  133.4 31.8 all-reduce.2
where the time goes:
time: 177 us
  waiting for transfers between devices  130 us (73%)
  matrix products  16.5 us (9%)
  between operations  15.2 us (9%)
  local copies, waits for them, and re-layouts  8.78 us (5%)
  starting transfers between devices  6.19 us (3%)
    psum x4, waiting for transfers between devices, visit(): summed = lax.psum(part, 'pw')  130 us
    dot_general x4, matrix products, visit(): jnp.dot(summed.astype(jnp.bfloat16), piece, preferred_element_type=jnp.fl...  10.2 us
    dot_general x4, matrix products, visit(): lax.dot_general(rows, piece, (((1,), (1,)), ((), ())), preferred_element_...  6.32 us
    ppermute x3, starting transfers between devices, from_behind(): return lax.ppermute(block, axis, route)  6.18 us
    dynamic_update_slice x4, local copies, waits for them, and re-layouts, visit(): lax.dynamic_update_slice(correlation, summed, (zero_index, start))  5.54 us
  transfers between devices with their start and end apart: 7, of which 4 were waited for; matrix products, arithmetic and copies ran while one was open for 9% of the time, Pallas kernels for 0%

commit v1 on v0

--- a/solution.py
+++ b/solution.py
@@ -1,7 +1,21 @@
+import functools
 import jax
 import jax.numpy as jnp
 from jax import lax
 from jax.sharding import PartitionSpec as P
+
+
+def _detail_region(chunk, dev_axis):
+    n_blocks = lax.axis_size(dev_axis)
+    ready = chunk
+    for w in [
+        [(kk, kk ^ dd) for kk in range(n_blocks)] for dd in (1, 2, 4, 8, 16) if dd < n_blocks
+    ]:
+        ready = ready + lax.ppermute(ready, dev_axis, w)
+    return ready
+
+
+scan_field_up = functools.partial(_detail_region, dev_axis="pw")
 
 
 def from_behind(block, axis, distance):
@@ -26,7 +40,7 @@
         part = lax.dot_general(
             rows, piece, (((1,), (1,)), ((), ())), preferred_element_type=jnp.float32
         )
-        summed = lax.psum(part, "pw")
+        summed = scan_field_up(part)
         correlation = lax.dynamic_update_slice(correlation, summed, (zero_index, start))
         correction = correction + jnp.dot(
             summed.astype(jnp.bfloat16), piece, preferred_element_type=jnp.float32

time: 177 us -> 132 us (0.75)
  waiting for transfers between devices: 130 us -> 101 us
  between operations: 15.2 us -> 0.69 us
  matrix products: 16.5 us -> 11.6 us
  starting transfers between devices: 6.19 us -> 9.08 us
  other arithmetic: 0.01 us -> 2.89 us
    psum x4 -> x0, waiting for transfers between devices: 130 us -> none  [visit(): summed = lax.psum(part, 'pw')]
    ppermute x3, waiting for transfers between devices: 0.01 us -> 72.4 us  [from_behind(): return lax.ppermute(block, axis, route)]
    ppermute x0 -> x8, waiting for transfers between devices: none -> 28.2 us  [_detail_region(): ready = ready + lax.ppermute(ready, dev_axis, w)]
    ppermute x0 -> x8, starting transfers between devices: none -> 5.86 us  [_detail_region(): ready = ready + lax.ppermute(ready, dev_axis, w)]
    dynamic_update_slice x4 -> x1, local copies, waits for them, and re-layouts: 5.54 us -> 1.62 us  [visit(): lax.dynamic_update_slice(correlation, summed, (zero_index, start))]
    ppermute x3, starting transfers between devices: 6.18 us -> 3.22 us  [from_behind(): return lax.ppermute(block, axis, route)]
    dot_general x4, matrix products: 6.32 us -> 3.41 us  [visit(): lax.dot_general(rows, piece, (((1,), (1,)), ((), ())), preferred_element_...]
    dynamic_update_slice x0 -> x3, other arithmetic: none -> 2.09 us  [visit(): lax.dynamic_update_slice(correlation, summed, (zero_index, start))]
  transfers between devices with their start and end apart: 7 -> 11, of which waited for: 4 -> 11; matrix products, arithmetic and copies ran while one was open for 9% -> 8% of each run, Pallas kernels for 0% -> 0%
where the time goes in v1:
time: 132 us
  waiting for transfers between devices  101 us (77%)
  matrix products  11.6 us (9%)
  starting transfers between devices  9.08 us (7%)
  local copies, waits for them, and re-layouts  7.12 us (5%)
  other arithmetic  2.89 us (2%)
    ppermute x3, waiting for transfers between devices, from_behind(): return lax.ppermute(block, axis, route)  72.4 us
    ppermute x8, waiting for transfers between devices, _detail_region(): ready = ready + lax.ppermute(ready, dev_axis, w)  28.2 us
    dot_general x4, matrix products, visit(): jnp.dot(summed.astype(jnp.bfloat16), piece, preferred_element_type=jnp.fl...  8.14 us
    ppermute x8, starting transfers between devices, _detail_region(): ready = ready + lax.ppermute(ready, dev_axis, w)  5.86 us
    dot_general x4, matrix products, visit(): lax.dot_general(rows, piece, (((1,), (1,)), ((), ())), preferred_element_...  3.41 us
    ppermute x3, starting transfers between devices, from_behind(): return lax.ppermute(block, axis, route)  3.22 us
  transfers between devices with their start and end apart: 11, of which 11 were waited for; matrix products, arithmetic and copies ran while one was open for 8% of the time, Pallas kernels for 0%

profile of v1, /device:TPU:0, one launch (start us, length us, event | category | flops | bytes accessed | tf_op | source)
XLA Modules:
  0.0 132.0 jit_solution(16636443213059432224)
XLA Ops:
  2.3 114.0 %while.20 = (s32[]{:T(128)}, bf16[384,2048]{1,0:T(8,128)(2,1)S(1)}, f32[128,1536]{1,0:T(8,128)}, f32[128,2048]{1,0:T(8,128)}, bf16[128,2048]{1,0:T(8,128)(2,1)},...) while((s32[]{:T(128)}, bf16[384,2048]{1,0:T(8,128)(2,1)S(1)}, ...), condition=%wide.region_1.2_spmd.clone, body=%wide.region_0.1_spmd.clone.sunk | while | flops 403374080 | bytes 20644284 | solution.py:56
  2.5 3.1 %collective-permute-start = (bf16[384,2048]{1,0:T(8,128)(2,1)S(1)}, bf16[384,2048]{1,0:T(8,128)(2,1)S(1)}, u32[]{:S(2)}, u32[]{:S(2)}) collective-permute-start(bf16[384,2048]{1,0:T(8,128)(2,1)S(1)} %copy.11), channel_id=1, source_target_pairs={{12,0},{0,4},{4,8},{8,12},{13,1},{1,5},{5,9},{9,13},{14,2},{2,6},{... | collective-permute-start | bytes 4718600 | tf_op jit(solution)/shard_map/while/body/eval_jaxpr/ppermute | solution.py:24
  6.3 1.4 %collective-permute-done.1 = f32[128,384]{1,0:T(8,128)S(1)} collective-permute-done((f32[128,384]{1,0:T(8,128)S(1)}, f32[128,384]{1,0:T(8,128)S(1)}, u32[]{:S(2)}, u32[]{:S(2)}) %collective-permute-start.1) | collective-permute-done | bytes 196640 | tf_op jit(solution)/shard_map/while/body/eval_jaxpr/ppermute | solution.py:14
  7.7 1.6 %collective-permute-start.2 = (f32[128,384]{1,0:T(8,128)S(1)}, f32[128,384]{1,0:T(8,128)S(1)}, u32[]{:S(2)}, u32[]{:S(2)}) collective-permute-start(f32[128,384]{1,0:T(8,128)S(1)} %add.127), channel_id=1, source_target_pairs={{0,2},{1,3},{2,0},{3,1},{4,6},{5,7},{6,4},{7,5},{8,10},{9,11},{10,... | collective-permute-start | bytes 589832 | tf_op jit(solution)/shard_map/while/body/eval_jaxpr/ppermute | solution.py:14
  9.3 5.5 %collective-permute-done.2 = f32[128,384]{1,0:T(8,128)S(1)} collective-permute-done((f32[128,384]{1,0:T(8,128)S(1)}, f32[128,384]{1,0:T(8,128)S(1)}, u32[]{:S(2)}, u32[]{:S(2)}) %collective-permute-start.2) | collective-permute-done | bytes 196640 | tf_op jit(solution)/shard_map/while/body/eval_jaxpr/ppermute | solution.py:14
  15.5 1.4 %convolution_add_fusion.3 = f32[128,2048]{1,0:T(8,128)} fusion(bf16[384,2048]{1,0:T(8,128)(2,1)S(1)} %copy.11, f32[128,2048]{1,0:T(8,128)} %get-tuple-element.247, pred[]{:T(512)S(6)} %compare.5, f32[128,384]{1,0:T(8,128)S(1)} %add.127, f32[128,384]{1,0:T(8,128)S(1)} %collective-permute-done.2), kind=kOutput, calls=%fused_computation.clone.1 | convolution fusion | flops 201949184 | bytes 4063233 | tf_op jit(solution)/shard_map/while/body/eval_jaxpr/dot_general | solution.py:45
  16.9 25.1 %collective-permute-done = bf16[384,2048]{1,0:T(8,128)(2,1)S(1)} collective-permute-done((bf16[384,2048]{1,0:T(8,128)(2,1)S(1)}, bf16[384,2048]{1,0:T(8,128)(2,1)S(1)}, u32[]{:S(2)}, u32[]{:S(2)}) %collective-permute-start) | collective-permute-done | bytes 1572896 | tf_op jit(solution)/shard_map/while/body/eval_jaxpr/ppermute | solution.py:24
  43.8 1.4 %collective-permute-done.1 = f32[128,384]{1,0:T(8,128)S(1)} collective-permute-done((f32[128,384]{1,0:T(8,128)S(1)}, f32[128,384]{1,0:T(8,128)S(1)}, u32[]{:S(2)}, u32[]{:S(2)}) %collective-permute-start.1) | collective-permute-done | bytes 196640 | tf_op jit(solution)/shard_map/while/body/eval_jaxpr/ppermute | solution.py:14
  45.2 1.6 %collective-permute-start.2 = (f32[128,384]{1,0:T(8,128)S(1)}, f32[128,384]{1,0:T(8,128)S(1)}, u32[]{:S(2)}, u32[]{:S(2)}) collective-permute-start(f32[128,384]{1,0:T(8,128)S(1)} %add.127), channel_id=1, source_target_pairs={{0,2},{1,3},{2,0},{3,1},{4,6},{5,7},{6,4},{7,5},{8,10},{9,11},{10,... | collective-permute-start | bytes 589832 | tf_op jit(solution)/shard_map/while/body/eval_jaxpr/ppermute | solution.py:14
  46.8 5.5 %collective-permute-done.2 = f32[128,384]{1,0:T(8,128)S(1)} collective-permute-done((f32[128,384]{1,0:T(8,128)S(1)}, f32[128,384]{1,0:T(8,128)S(1)}, u32[]{:S(2)}, u32[]{:S(2)}) %collective-permute-start.2) | collective-permute-done | bytes 196640 | tf_op jit(solution)/shard_map/while/body/eval_jaxpr/ppermute | solution.py:14
  52.9 2.6 %convolution_add_fusion.3 = f32[128,2048]{1,0:T(8,128)} fusion(bf16[384,2048]{1,0:T(8,128)(2,1)S(1)} %copy.11, f32[128,2048]{1,0:T(8,128)} %get-tuple-element.247, pred[]{:T(512)S(6)} %compare.5, f32[128,384]{1,0:T(8,128)S(1)} %add.127, f32[128,384]{1,0:T(8,128)S(1)} %collective-permute-done.2), kind=kOutput, calls=%fused_computation.clone.1 | convolution fusion | flops 201949184 | bytes 4063233 | tf_op jit(solution)/shard_map/while/body/eval_jaxpr/dot_general | solution.py:45
  55.6 24.1 %collective-permute-done = bf16[384,2048]{1,0:T(8,128)(2,1)S(1)} collective-permute-done((bf16[384,2048]{1,0:T(8,128)(2,1)S(1)}, bf16[384,2048]{1,0:T(8,128)(2,1)S(1)}, u32[]{:S(2)}, u32[]{:S(2)}) %collective-permute-start) | collective-permute-done | bytes 1572896 | tf_op jit(solution)/shard_map/while/body/eval_jaxpr/ppermute | solution.py:24
  81.3 1.4 %collective-permute-done.1 = f32[128,384]{1,0:T(8,128)S(1)} collective-permute-done((f32[128,384]{1,0:T(8,128)S(1)}, f32[128,384]{1,0:T(8,128)S(1)}, u32[]{:S(2)}, u32[]{:S(2)}) %collective-permute-start.1) | collective-permute-done | bytes 196640 | tf_op jit(solution)/shard_map/while/body/eval_jaxpr/ppermute | solution.py:14
  82.8 1.3 %collective-permute-start.2 = (f32[128,384]{1,0:T(8,128)S(1)}, f32[128,384]{1,0:T(8,128)S(1)}, u32[]{:S(2)}, u32[]{:S(2)}) collective-permute-start(f32[128,384]{1,0:T(8,128)S(1)} %add.127), channel_id=1, source_target_pairs={{0,2},{1,3},{2,0},{3,1},{4,6},{5,7},{6,4},{7,5},{8,10},{9,11},{10,... | collective-permute-start | bytes 589832 | tf_op jit(solution)/shard_map/while/body/eval_jaxpr/ppermute | solution.py:14
  84.1 5.7 %collective-permute-done.2 = f32[128,384]{1,0:T(8,128)S(1)} collective-permute-done((f32[128,384]{1,0:T(8,128)S(1)}, f32[128,384]{1,0:T(8,128)S(1)}, u32[]{:S(2)}, u32[]{:S(2)}) %collective-permute-start.2) | collective-permute-done | bytes 196640 | tf_op jit(solution)/shard_map/while/body/eval_jaxpr/ppermute | solution.py:14
  90.5 2.6 %convolution_add_fusion.3 = f32[128,2048]{1,0:T(8,128)} fusion(bf16[384,2048]{1,0:T(8,128)(2,1)S(1)} %copy.11, f32[128,2048]{1,0:T(8,128)} %get-tuple-element.247, pred[]{:T(512)S(6)} %compare.5, f32[128,384]{1,0:T(8,128)S(1)} %add.127, f32[128,384]{1,0:T(8,128)S(1)} %collective-permute-done.2), kind=kOutput, calls=%fused_computation.clone.1 | convolution fusion | flops 201949184 | bytes 4063233 | tf_op jit(solution)/shard_map/while/body/eval_jaxpr/dot_general | solution.py:45
  93.1 23.2 %collective-permute-done = bf16[384,2048]{1,0:T(8,128)(2,1)S(1)} collective-permute-done((bf16[384,2048]{1,0:T(8,128)(2,1)S(1)}, bf16[384,2048]{1,0:T(8,128)(2,1)S(1)}, u32[]{:S(2)}, u32[]{:S(2)}) %collective-permute-start) | collective-permute-done | bytes 1572896 | tf_op jit(solution)/shard_map/while/body/eval_jaxpr/ppermute | solution.py:24
  116.3 1.6 %convolution_bitcast_fusion = f32[128,384]{0,1:T(8,128)S(1)} fusion(bf16[384,2048]{1,0:T(8,128)(2,1)S(1)} %get-tuple-element.160, bf16[1,128,2048]{2,1,0:T(8,128)(2,1)} %bitcast.23), kind=kOutput, calls=%fused_computation.7 | convolution fusion | flops 201326592 | bytes 2293760 | tf_op jit(solution)/shard_map/dot_general | solution.py:40
  118.1 1.4 %collective-permute-done.3 = f32[128,384]{0,1:T(8,128)S(1)} collective-permute-done((f32[128,384]{0,1:T(8,128)S(1)}, f32[128,384]{0,1:T(8,128)S(1)}, u32[]{:S(2)}, u32[]{:S(2)}) %collective-permute-start.3) | collective-permute-done | bytes 196640 | tf_op jit(solution)/shard_map/ppermute | solution.py:14
  119.5 1.1 collective-permute-start.4
  120.6 5.9 %collective-permute-done.4 = f32[128,384]{0,1:T(8,128)S(1)} collective-permute-done((f32[128,384]{0,1:T(8,128)S(1)}, f32[128,384]{0,1:T(8,128)S(1)}, u32[]{:S(2)}, u32[]{:S(2)}) %collective-permute-start.4) | collective-permute-done | bytes 196640 | tf_op jit(solution)/shard_map/ppermute | solution.py:14
  127.2 1.7 %copy.4 = f32[1,128,384]{2,1,0:T(8,128)} copy(f32[1,128,384]{1,2,0:T(8,128)} %add_bitcast_fusion) | data formatting | bytes 393216 | tf_op jit(solution)/shard_map/reshape | solution.py:61
  128.9 1.6 %constant_dynamic-update-slice_fusion = f32[1,128,1536]{2,1,0:T(8,128)} fusion(f32[1,128,1536]{2,1,0:T(8,128)} %bitcast.25, f32[1,128,384]{2,1,0:T(8,128)} %copy.4, s32[]{:T(128)S(6)} %select_n.38), kind=kLoop, calls=%fused_computation.11 | loop fusion | bytes 393220 | tf_op jit(solution)/shard_map/dynamic_update_slice | solution.py:44
  130.6 1.4 %fusion.3 = f32[1,128,2048]{2,1,0:T(8,128)} fusion(f32[128,2048]{1,0:T(8,128)S(1)} %copy-done.1, bf16[384,2048]{1,0:T(8,128)(2,1)S(1)} %get-tuple-element.160, f32[128,384]{0,1:T(8,128)S(1)} %add.87, f32[128,384]{0,1:T(8,128)S(1)} %collective-permute-done.4, bf16[1,128,2048]{2,1,0:T(8,128)(2,1)S(1)} %bitcast.24), kind=kOutput, calls=%fused_computation.6 | convolution fusion | flops 202211328 | bytes 4587520 | tf_op jit(solution)/shard_map/dot_general | solution.py:45
  (34 shorter events, 8.9 us)
Async XLA Ops:
  0.6 1.7 %copy-start = (bf16[384,2048]{1,0:T(8,128)(2,1)S(1)}, bf16[384,2048]{1,0:T(8,128)(2,1)}, u32[]{:S(2)}) copy-start(bf16[384,2048]{1,0:T(8,128)(2,1)} %param.4) | copy-start | bytes 4718596
  2.3 3.3 %copy-start.2 = (bf16[128,2048]{1,0:T(8,128)(2,1)S(1)}, bf16[128,2048]{1,0:T(8,128)(2,1)}, u32[]{:S(2)}) copy-start(bf16[128,2048]{1,0:T(8,128)(2,1)} %get-tuple-element.260) | copy-start | bytes 1572868 | tf_op jit(solution)/shard_map/while
  2.5 39.5 %collective-permute-start = (bf16[384,2048]{1,0:T(8,128)(2,1)S(1)}, bf16[384,2048]{1,0:T(8,128)(2,1)S(1)}, u32[]{:S(2)}, u32[]{:S(2)}) collective-permute-start(bf16[384,2048]{1,0:T(8,128)(2,1)S(1)} %copy.11), channel_id=1, source_target_pairs={{12,0},{0,4},{4,8},{8,12},{13,1},{1,5},{5,9},{9,13},{14,2},{2,6},{... | collective-permute-start | bytes 4718600 | tf_op jit(solution)/shard_map/while/body/eval_jaxpr/ppermute | solution.py:24
  6.2 1.5 %collective-permute-start.1 = (f32[128,384]{1,0:T(8,128)S(1)}, f32[128,384]{1,0:T(8,128)S(1)}, u32[]{:S(2)}, u32[]{:S(2)}) collective-permute-start(f32[128,384]{1,0:T(8,128)S(1)} %fusion.22), channel_id=1, source_target_pairs={{0,1},{1,0},{2,3},{3,2},{4,5},{5,4},{6,7},{7,6},{8,9},{9,8},{10,11... | collective-permute-start | bytes 589832 | tf_op jit(solution)/shard_map/while/body/eval_jaxpr/ppermute | solution.py:14
  7.7 7.0 %collective-permute-start.2 = (f32[128,384]{1,0:T(8,128)S(1)}, f32[128,384]{1,0:T(8,128)S(1)}, u32[]{:S(2)}, u32[]{:S(2)}) collective-permute-start(f32[128,384]{1,0:T(8,128)S(1)} %add.127), channel_id=1, source_target_pairs={{0,2},{1,3},{2,0},{3,1},{4,6},{5,7},{6,4},{7,5},{8,10},{9,11},{10,... | collective-permute-start | bytes 589832 | tf_op jit(solution)/shard_map/while/body/eval_jaxpr/ppermute | solution.py:14
  42.0 1.0 copy-start.2
  42.2 37.4 %collective-permute-start = (bf16[384,2048]{1,0:T(8,128)(2,1)S(1)}, bf16[384,2048]{1,0:T(8,128)(2,1)S(1)}, u32[]{:S(2)}, u32[]{:S(2)}) collective-permute-start(bf16[384,2048]{1,0:T(8,128)(2,1)S(1)} %copy.11), channel_id=1, source_target_pairs={{12,0},{0,4},{4,8},{8,12},{13,1},{1,5},{5,9},{9,13},{14,2},{2,6},{... | collective-permute-start | bytes 4718600 | tf_op jit(solution)/shard_map/while/body/eval_jaxpr/ppermute | solution.py:24
  43.7 1.5 %collective-permute-start.1 = (f32[128,384]{1,0:T(8,128)S(1)}, f32[128,384]{1,0:T(8,128)S(1)}, u32[]{:S(2)}, u32[]{:S(2)}) collective-permute-start(f32[128,384]{1,0:T(8,128)S(1)} %fusion.22), channel_id=1, source_target_pairs={{0,1},{1,0},{2,3},{3,2},{4,5},{5,4},{6,7},{7,6},{8,9},{9,8},{10,11... | collective-permute-start | bytes 589832 | tf_op jit(solution)/shard_map/while/body/eval_jaxpr/ppermute | solution.py:14
  45.2 7.0 %collective-permute-start.2 = (f32[128,384]{1,0:T(8,128)S(1)}, f32[128,384]{1,0:T(8,128)S(1)}, u32[]{:S(2)}, u32[]{:S(2)}) collective-permute-start(f32[128,384]{1,0:T(8,128)S(1)} %add.127), channel_id=1, source_target_pairs={{0,2},{1,3},{2,0},{3,1},{4,6},{5,7},{6,4},{7,5},{8,10},{9,11},{10,... | collective-permute-start | bytes 589832 | tf_op jit(solution)/shard_map/while/body/eval_jaxpr/ppermute | solution.py:14
  79.6 1.0 copy-start.2
  79.8 36.6 %collective-permute-start = (bf16[384,2048]{1,0:T(8,128)(2,1)S(1)}, bf16[384,2048]{1,0:T(8,128)(2,1)S(1)}, u32[]{:S(2)}, u32[]{:S(2)}) collective-permute-start(bf16[384,2048]{1,0:T(8,128)(2,1)S(1)} %copy.11), channel_id=1, source_target_pairs={{12,0},{0,4},{4,8},{8,12},{13,1},{1,5},{5,9},{9,13},{14,2},{2,6},{... | collective-permute-start | bytes 4718600 | tf_op jit(solution)/shard_map/while/body/eval_jaxpr/ppermute | solution.py:24
  81.3 1.5 %collective-permute-start.1 = (f32[128,384]{1,0:T(8,128)S(1)}, f32[128,384]{1,0:T(8,128)S(1)}, u32[]{:S(2)}, u32[]{:S(2)}) collective-permute-start(f32[128,384]{1,0:T(8,128)S(1)} %fusion.22), channel_id=1, source_target_pairs={{0,1},{1,0},{2,3},{3,2},{4,5},{5,4},{6,7},{7,6},{8,9},{9,8},{10,11... | collective-permute-start | bytes 589832 | tf_op jit(solution)/shard_map/while/body/eval_jaxpr/ppermute | solution.py:14
  82.8 7.0 %collective-permute-start.2 = (f32[128,384]{1,0:T(8,128)S(1)}, f32[128,384]{1,0:T(8,128)S(1)}, u32[]{:S(2)}, u32[]{:S(2)}) collective-permute-start(f32[128,384]{1,0:T(8,128)S(1)} %add.127), channel_id=1, source_target_pairs={{0,2},{1,3},{2,0},{3,1},{4,6},{5,7},{6,4},{7,5},{8,10},{9,11},{10,... | collective-permute-start | bytes 589832 | tf_op jit(solution)/shard_map/while/body/eval_jaxpr/ppermute | solution.py:14
  117.9 12.6 %copy-start.1 = (f32[128,2048]{1,0:T(8,128)S(1)}, f32[128,2048]{1,0:T(8,128)}, u32[]{:S(2)}) copy-start(f32[128,2048]{1,0:T(8,128)} %get-tuple-element.161) | copy-start | bytes 3145732
  118.0 12.6 %copy-start.3 = (bf16[128,2048]{1,0:T(8,128)(2,1)S(1)}, bf16[128,2048]{1,0:T(8,128)(2,1)}, u32[]{:S(2)}) copy-start(bf16[128,2048]{1,0:T(8,128)(2,1)} %get-tuple-element.271) | copy-start | bytes 1572868
  118.0 1.5 %collective-permute-start.3 = (f32[128,384]{0,1:T(8,128)S(1)}, f32[128,384]{0,1:T(8,128)S(1)}, u32[]{:S(2)}, u32[]{:S(2)}) collective-permute-start(f32[128,384]{0,1:T(8,128)S(1)} %convolution_bitcast_fusion), channel_id=1, source_target_pairs={{0,1},{1,0},{2,3},{3,2},{4,5},{5,4},{6,7},{7,6},{8,9},{9,8},{10,11... | collective-permute-start | bytes 589832 | tf_op jit(solution)/shard_map/ppermute | solution.py:14
  119.5 7.0 %collective-permute-start.4 = (f32[128,384]{0,1:T(8,128)S(1)}, f32[128,384]{0,1:T(8,128)S(1)}, u32[]{:S(2)}, u32[]{:S(2)}) collective-permute-start(f32[128,384]{0,1:T(8,128)S(1)} %add.87), channel_id=1, source_target_pairs={{0,2},{1,3},{2,0},{3,1},{4,6},{5,7},{6,4},{7,5},{8,10},{9,11},{10,... | collective-permute-start | bytes 589832 | tf_op jit(solution)/shard_map/ppermute | solution.py:14
